TPU v7x, 128 devices: a whole 4x4x4 slice. The times are simulated.
128 devices in a mesh: dp: 16 (over z, y_lo, core), expert: 8 (over x, y_hi).
Axes of the slice: x: 4, y: 4 (y_hi: 2, y_lo: 2; y = y_hi * 2 + y_lo), z: 4, core: 2. Of those that a mesh axis runs over, the one named last changes fastest.
Arguments:
- tokens: bfloat16 [16384, 4096], P(('dp', 'expert')), may hold values from -6 to 6
- expert_ids: int32 [16384, 2], P(('dp', 'expert')), may hold values from 0 to 7, all different within a row; in each aligned block of 128 rows (0 to 127, 128 to 255, ...) at most 80 rows name the same one
- gate_probs: float32 [16384, 2], P(('dp', 'expert')), may hold values from 0.2 to 1
- gate_weight: bfloat16 [8, 4096, 1536], P('expert', 'dp'), may hold values from -0.09375 to 0.09375
- up_weight: bfloat16 [8, 4096, 1536], P('expert', 'dp'), may hold values from -0.09375 to 0.09375
- down_weight: bfloat16 [8, 1536, 4096], P('expert', None, 'dp'), may hold values from -0.15625 to 0.15625
Outputs:
- mixed: bfloat16 [16384, 4096], P(('dp', 'expert'))
Inputs may be any that keep to these rules, and one draw needn't show every extreme that they name: `expert_ids`: each token names 2 different experts. Among the 128 tokens of one device (aligned blocks of rows), no expert is named by more than 80 tokens, and in every draw some expert is named by exactly 80 tokens of some device.
All inputs are finite; a program needn't handle non-finite values.
Results may differ from a plain program's by a relative error of at most 0.0057.
Values may be sent and summed in bfloat16 or wider, within the bound.
A program may use at most 128 MiB of HBM per device.

v0:
```python
import jax
import jax.numpy as jnp
from jax import lax
from jax.sharding import PartitionSpec as P

CAP = 80


def on_device(tokens, expert_ids, gate_probs, gate_weight, up_weight, down_weight):
    tok_count, model_width = tokens.shape
    top_count = expert_ids.shape[1]
    groups = lax.axis_size("expert")
    total_rows = groups * CAP
    flat_ids = expert_ids.reshape(-1)
    onehot = (flat_ids[:, None] == jnp.arange(groups, dtype=jnp.int32)[None, :]).astype(jnp.int32)
    ranks = jnp.cumsum(onehot, axis=0) - 1
    rank_own = jnp.sum(ranks * onehot, axis=1)
    slot_index = flat_ids * CAP + rank_own
    counts = jnp.sum(onehot, axis=0)
    source_rows = jnp.arange(tok_count * top_count, dtype=jnp.int32) // top_count
    table = jnp.full((total_rows,), tok_count, jnp.int32).at[slot_index].set(source_rows)
    padded_tokens = jnp.concatenate([tokens, jnp.zeros((1, model_width), tokens.dtype)], axis=0)
    send_rows = padded_tokens[table]
    received, arrived = (
        lax.all_to_all(send_rows, "expert", split_axis=0, concat_axis=0, tiled=True),
        lax.all_to_all(counts[:, None], "expert", split_axis=0, concat_axis=0, tiled=True),
    )
    arrived = arrived[:, 0]
    gate_local = gate_weight[0]
    up_local = up_weight[0]
    down_local = down_weight[0]
    gate = jnp.dot(
        received,
        lax.all_gather(gate_local, "dp", axis=0, tiled=True),
        preferred_element_type=jnp.float32,
    )
    upper = jnp.dot(
        received,
        lax.all_gather(up_local, "dp", axis=0, tiled=True),
        preferred_element_type=jnp.float32,
    )
    hidden = (jax.nn.silu(gate) * upper).astype(jnp.bfloat16)
    outputs = jnp.dot(
        hidden,
        lax.all_gather(down_local, "dp", axis=1, tiled=True),
        preferred_element_type=jnp.float32,
    ).astype(jnp.bfloat16)
    returned = lax.all_to_all(outputs, "expert", split_axis=0, concat_axis=0, tiled=True)
    picked = returned[slot_index].astype(jnp.float32)
    weighted = picked * gate_probs.reshape(-1)[:, None]
    mixed = jnp.sum(weighted.reshape(tok_count, top_count, model_width), axis=1)
    return mixed.astype(jnp.bfloat16)


def solution(mesh):
    placed = (
        P(("dp", "expert"), None),
        P(("dp", "expert"), None),
        P(("dp", "expert"), None),
        P("expert", "dp", None),
        P("expert", "dp", None),
        P("expert", None, "dp"),
    )
    return jax.shard_map(
        on_device, mesh=mesh, in_specs=placed, out_specs=P(("dp", "expert"), None), check_vma=False
    )
```

profile of v0, /device:TPU:0, one launch (start us, length us, event | category | flops | bytes accessed | tf_op | source)
XLA Modules:
  0.0 431.1 jit_solution(3689289020772454636)
XLA Ops:
  6.5 0.0 all-gather.7.cloned.1.call-start
  6.5 0.7 all-gather.7.cloned.1.call-update
  7.3 0.0 all-gather.11.cloned.1.call-start
  7.3 0.7 all-gather.11.cloned.1.call-update
  8.0 0.0 all-gather.9.cloned.1.call-start
  8.1 0.7 all-gather.9.cloned.1.call-update
  8.7 0.8 copy.9
  9.5 0.1 eq.29
  9.7 0.1 eq.25
  9.8 0.6 reduce-window.6
  10.4 0.2 slice_reduce_fusion
  10.7 0.7 broadcast_multiply_fusion
  11.4 0.1 copy.8
  11.5 0.1 mul.37
  11.6 1.3 concatenate.3
  13.0 0.1 fusion.14
  13.1 0.0 copy-start
  13.1 1.4 scatter_custom_fusion
  14.5 5.4 %gather_fusion = bf16[640,4096]{1,0:T(8,128)(2,1)} fusion(bf16[129,4096]{1,0:T(8,128)(2,1)S(1)} %concatenate.3, s32[1024]{0:T(1024)S(1)} %pad_clamp_fusion.1), kind=kCustom, calls=%fused_computation | custom fusion | bytes 10488320 | tf_op jit(solution)/shard_map/gather | solution.py:23
  19.9 0.0 copy-done
  19.9 82.1 %all_to_all.24 = bf16[8,80,4096]{2,1,0:T(8,128)(2,1)} all-to-all(bf16[8,80,4096]{2,1,0:T(8,128)(2,1)} %bitcast.29), channel_id=1, replica_groups=mesh['dp'=16,'expert'=8] {'expert'}, dimensions={0} | all-to-all | bytes 10485760 | tf_op jit(solution)/shard_map/all_to_all | solution.py:25
  102.0 37.5 %all-gather.7.cloned.1.call-done = bf16[1,4096,1536]{2,1,0:T(8,128)(2,1)} async-done(((bf16[1,256,1536]{2,1,0:T(8,128)(2,1)}), bf16[1,4096,1536]{2,1,0:T(8,128)(2,1)}) %all-gather.7.cloned.1.call-update) | async-done | bytes 12582928 | tf_op jit(solution)/shard_map/all_gather | solution.py:34
  139.5 14.1 %fusion.4 = f32[640,1536]{1,0:T(8,128)} fusion(bf16[640,4096]{1,0:T(8,128)(2,1)} %bitcast.30, bf16[1,4096,1536]{2,1,0:T(8,128)(2,1)} %all-gather.7.cloned.1.call-done), kind=kOutput, calls=%fused_computation.7 | convolution fusion | flops 8053063680 | bytes 21757952 | tf_op jit(solution)/shard_map/dot_general | solution.py:32
  153.5 67.9 %all-gather.11.cloned.1.call-done = bf16[1,1536,4096]{2,1,0:T(8,128)(2,1)} async-done(((bf16[1,1536,256]{2,1,0:T(8,128)(2,1)}), bf16[1,1536,4096]{2,1,0:T(8,128)(2,1)}) %all-gather.11.cloned.1.call-update) | async-done | bytes 12582928 | tf_op jit(solution)/shard_map/all_gather | solution.py:45
  221.5 73.6 %all-gather.9.cloned.1.call-done = bf16[1,4096,1536]{2,1,0:T(8,128)(2,1)} async-done(((bf16[1,256,1536]{2,1,0:T(8,128)(2,1)}), bf16[1,4096,1536]{2,1,0:T(8,128)(2,1)}) %all-gather.9.cloned.1.call-update) | async-done | bytes 12582928 | tf_op jit(solution)/shard_map/all_gather | solution.py:39
  295.1 27.9 %fusion.6 = bf16[640,4096]{1,0:T(8,128)(2,1)} fusion(bf16[1,1536,4096]{2,1,0:T(8,128)(2,1)} %all-gather.11.cloned.1.call-done, f32[640,1536]{1,0:T(8,128)} %fusion.4, bf16[640,4096]{1,0:T(8,128)(2,1)} %bitcast.31, bf16[1,4096,1536]{2,1,0:T(8,128)(2,1)} %all-gather.9.cloned.1.call-done), kind=kOutput, calls=%fused_computation.9 | convolution fusion | flops 16114647040 | bytes 39583744 | tf_op jit(solution)/shard_map/dot_general | solution.py:43
  322.9 0.0 copy-start.2
  322.9 0.0 copy-start.1
  322.9 6.8 %all-to-all-start.1 = ((bf16[8,80,4096]{2,1,0:T(8,128)(2,1)}), bf16[8,80,4096]{2,1,0:T(8,128)(2,1)}, u32[]{:S(2)}, u32[]{:S(2)}) async-start(bf16[8,80,4096]{2,1,0:T(8,128)(2,1)} %bitcast.32), calls=%async_computation.1 | async-start | bytes 10485760 | tf_op jit(solution)/shard_map/all_to_all | solution.py:48
  329.8 0.0 copy-done.2
  329.8 0.1 copy.11
  329.9 0.0 copy-done.1
  329.9 73.9 %all-to-all-done.1 = bf16[8,80,4096]{2,1,0:T(8,128)(2,1)} async-done(((bf16[8,80,4096]{2,1,0:T(8,128)(2,1)}), bf16[8,80,4096]{2,1,0:T(8,128)(2,1)}, u32[]{:S(2)}, u32[]{:S(2)}) %all-to-all-start.1) | async-done | bytes 5242912 | tf_op jit(solution)/shard_map/all_to_all | solution.py:48
  403.8 7.0 %gather_fusion.1 = bf16[256,4096]{1,0:T(8,128)(2,1)S(1)} fusion(bf16[640,4096]{1,0:T(8,128)(2,1)} %bitcast.10, s32[1024]{0:T(1024)S(1)} %pad_clamp_fusion), kind=kCustom, calls=%fused_computation.1 | custom fusion | bytes 4195328 | tf_op jit(solution)/shard_map/gather | solution.py:49
  410.9 4.0 reshape.63
  414.9 9.6 %multiply_reduce_fusion = bf16[128,4096]{1,0:T(8,128)(2,1)} fusion(f32[128,2,4096]{2,1,0:T(2,128)} %reshape.63, f32[128,2]{1,0:T(8,128)S(1)} %copy.11), kind=kLoop, calls=%fused_computation.10 | loop fusion | flops 1572864 | bytes 5243904 | tf_op jit(solution)/shard_map/reduce_sum | solution.py:51
  (8 shorter events, 0.1 us)
Async XLA Ops:
  6.5 132.9 %all-gather.7.cloned.1.call-start = ((), (), s32[]{:S(2)}) async-start(), calls=%async_computation.2 | async-start | bytes 13369344 | tf_op jit(solution)/shard_map/all_gather | solution.py:34
  7.3 214.2 %all-gather.11.cloned.1.call-start = ((), (), s32[]{:S(2)}) async-start(), calls=%async_computation.4 | async-start | bytes 13369344 | tf_op jit(solution)/shard_map/all_gather | solution.py:45
  8.0 287.1 %all-gather.9.cloned.1.call-start = ((), (), s32[]{:S(2)}) async-start(), calls=%async_computation.3 | async-start | bytes 13369344 | tf_op jit(solution)/shard_map/all_gather | solution.py:39
  13.1 6.9 %copy-start = (s32[256,1]{0,1:T(1,128)}, s32[256,1]{0,1:T(1,128)S(1)}, u32[]{:S(2)}) copy-start(s32[256,1]{0,1:T(1,128)S(1)} %compare_select_fusion.1) | copy-start | bytes 3076
  322.9 6.9 %copy-start.2 = (f32[128,2]{0,1:T(2,128)S(1)}, f32[128,2]{0,1:T(2,128)}, u32[]{:S(2)}) copy-start(f32[128,2]{0,1:T(2,128)} %param.8) | copy-start | bytes 3076
  322.9 7.0 %copy-start.1 = (s32[256,1]{0,1:T(1,128)S(1)}, s32[256,1]{0,1:T(1,128)}, u32[]{:S(2)}) copy-start(s32[256,1]{0,1:T(1,128)} %copy-done) | copy-start | bytes 3076
  322.9 80.9 %all-to-all-start.1 = ((bf16[8,80,4096]{2,1,0:T(8,128)(2,1)}), bf16[8,80,4096]{2,1,0:T(8,128)(2,1)}, u32[]{:S(2)}, u32[]{:S(2)}) async-start(bf16[8,80,4096]{2,1,0:T(8,128)(2,1)} %bitcast.32), calls=%async_computation.1 | async-start | bytes 10485760 | tf_op jit(solution)/shard_map/all_to_all | solution.py:48
Sparse Core Ops, SparseCore 0:
  9.1 130.3 all-gather.6
  141.1 80.3 all-gather.10
  223.2 71.8 all-gather.8
where the time goes:
time: 432 us; the launch traced here: 431 us
  waiting for transfers between devices  255 us (59%)
  blocking collectives  82.1 us (19%)
  matrix products  41.9 us (10%)
  local copies, waits for them, and re-layouts  20.8 us (5%)
  between operations  13.2 us (3%)
  other arithmetic  11.1 us (3%)
  starting transfers between devices  6.92 us (2%)
    all_to_all x1, blocking collectives, on_device(): lax.all_to_all(send_rows, 'expert', split_axis=0, concat_axis=0, tiled=True)  82.1 us
    all_to_all x1, waiting for transfers between devices, on_device(): lax.all_to_all(outputs, 'expert', split_axis=0, concat_axis=0, tiled=True)  73.9 us
    all_gather x1, waiting for transfers between devices, on_device(): lax.all_gather(up_local, 'dp', axis=0, tiled=True)  73.6 us
    all_gather x1, waiting for transfers between devices, on_device(): lax.all_gather(down_local, 'dp', axis=1, tiled=True)  67.9 us
    all_gather x1, waiting for transfers between devices, on_device(): lax.all_gather(gate_local, 'dp', axis=0, tiled=True)  37.5 us
    dot_general x1, matrix products, on_device(): jnp.dot(hidden, lax.all_gather(down_local, 'dp', axis=1, tiled=True), pre...  27.9 us
    dot_general x1, matrix products, on_device(): jnp.dot(received, lax.all_gather(gate_local, 'dp', axis=0, tiled=True), p...  14.1 us
    reduce_sum x1, other arithmetic, on_device(): mixed = jnp.sum(weighted.reshape(tok_count, top_count, model_width), axis=1)  9.64 us
  transfers between devices with their start and end apart: 4, of which 4 were waited for; matrix products, arithmetic and copies ran while one was open for 6% of the time, Pallas kernels for 0%

commit v1 on v0

v1 whole, which is shorter than its diff:
```python
import jax
import jax.numpy as jnp
from jax import lax
from jax.experimental import pallas as pl
from jax.experimental.pallas import tpu as pltpu
from jax.sharding import PartitionSpec as P

CAP = 80
MESH = pl.DeviceIdType.MESH
COPIES = 120

def slot(dz, dy):
    return (dz % 4) * 2 + dy


def kernel(tok_hbm, meta_ref, gate_hbm, up_hbm, down_hbm, out_ref,
           gate_buf, up_buf, down_buf, gate_acc, up_acc, rows, hidden, own_tok, peer_tok, peer_meta,
           back, lanes, part_send, part_recv, mix, ssem, rsem, lsem):
    dp = lax.axis_index("dp")
    ex = lax.axis_index("expert")
    core, y, z = dp % 2, (dp // 2) % 2, dp // 4
    x, h = ex // 2, ex % 2

    def device(x_, h_, z_, y_, c_):
        return (z_ * 4 + y_ * 2 + c_, x_ * 2 + h_)

    z_up, z_down = device(x, h, (z + 1) % 4, y, core), device(x, h, (z + 3) % 4, y, core)
    y_in = device(x, h, z, 1 - y, core)
    sibling = device(x, h, z, y, 1 - core)
    y_out = device(x, 1 - h, z, 1 - y, core)
    x_by = [device((x + d) % 4, h, z, y, core) for d in range(4)]

    partners = (z_up, z_down, y_in, sibling, y_out, x_by[1], x_by[2], x_by[3])
    barrier = pltpu.get_barrier_semaphore()
    load_own = pltpu.make_async_copy(tok_hbm, own_tok.at[pl.ds(0, 128), :], lsem.at[3])
    load_own.start()
    for partner in partners:
        pl.semaphore_signal(barrier, inc=1, device_id=partner, device_id_type=MESH)
    pl.semaphore_wait(barrier, len(partners))

    sends = []

    def send(src, dst, dev):
        i = len(sends)
        copy = pltpu.make_async_remote_copy(
            src_ref=src, dst_ref=dst, send_sem=ssem.at[i], recv_sem=rsem.at[i],
            device_id=dev, device_id_type=MESH)
        copy.start()
        sends.append(copy)
        return i

    def arrive(i, dst):
        pltpu.make_async_remote_copy(
            src_ref=dst, dst_ref=dst, send_sem=ssem.at[i], recv_sem=rsem.at[i],
            device_id=sibling, device_id_type=MESH).wait_recv()

    args = (gate_hbm.at[0], up_hbm.at[0], down_hbm.at[0])
    bufs = (gate_buf, up_buf, down_buf)
    sizes = (256, 256, 1536)
    extra = (48, 48, 256)
    events = {}
    local = []

    def span(ref, lo, hi):
        return ref.at[pl.ds(lo, hi - lo), :]

    def push(m, key, src, r, lo, hi, dev):
        i = send(span(src, lo, hi), span(bufs[m].at[r, core], lo, hi), dev)
        events[m, key] = (i, r, lo, hi)

    def take(m, key, who):
        i, r, lo, hi = events[m, key]
        arrive(i, span(bufs[m].at[r, who], lo, hi))

    def pass_on(m, key):
        i, r, lo, hi = events[m, key]
        take(m, key, core)
        push(m, "s" + key, bufs[m].at[r, core], r, lo, hi, sibling)

    def start_own(m):
        n = sizes[m]
        push(m, "y", args[m], slot(0, 1), 0, n, y_in)
        push(m, "zu", args[m], slot(3, 0), 0, n, z_up)
        push(m, "zd", args[m], slot(1, 0), 0, n, z_down)
        push(m, "sown", args[m], slot(0, 0), 0, n, sibling)
        copy = pltpu.make_async_copy(args[m], bufs[m].at[slot(0, 0), core], lsem.at[m])
        copy.start()
        local.append(copy)

    def hop_two(m):
        n = sizes[m]
        cut = n - extra[m]
        for key, dz, lo, hi, dev in (("zu", 3, 0, n // 2, z_up), ("zd", 1, n // 2, n, z_down)):
            take(m, key, core)
            src = bufs[m].at[slot(dz, 0), core]
            push(m, "2" + key, src, slot(2, 0), lo, hi, dev)
            push(m, "q" + key, src, slot(dz, 1), cut, n, y_in)
            push(m, "s" + key, src, slot(dz, 0), 0, n, sibling)
        take(m, "y", core)
        src = bufs[m].at[slot(0, 1), core]
        push(m, "yzu", src, slot(3, 1), 0, cut, z_up)
        push(m, "yzd", src, slot(1, 1), 0, cut, z_down)
        push(m, "sy", src, slot(0, 1), 0, n, sibling)

    def hop_three(m):
        for key in ("2zu", "2zd"):
            i, r, lo, hi = events[m, key]
            take(m, key, core)
            push(m, "y" + key, bufs[m].at[r, core], slot(2, 1), lo, hi, y_in)
            push(m, "s" + key, bufs[m].at[r, core], r, lo, hi, sibling)
        for key in ("qzu", "qzd", "yzu", "yzd"):
            pass_on(m, key)

    def hop_four(m):
        pass_on(m, "y2zu")
        pass_on(m, "y2zd")

    from_sibling = {
        slot(0, 0): ("sown",), slot(0, 1): ("sy",), slot(3, 0): ("szu",), slot(1, 0): ("szd",),
        slot(2, 0): ("s2zu", "s2zd"), slot(3, 1): ("sqzu", "syzu"), slot(1, 1): ("sqzd", "syzd"),
        slot(2, 1): ("sy2zu", "sy2zd")}

    def whole_slot(m, r):
        if r == slot(0, 0):
            local[m].wait()
        for key in from_sibling[r]:
            take(m, key, 1 - core)

    later = (lax.broadcasted_iota(jnp.int32, (128, 128), 0)
             < lax.broadcasted_iota(jnp.int32, (128, 128), 1)).astype(jnp.bfloat16)
    place = lax.broadcasted_iota(jnp.int32, (CAP, 128), 0).astype(jnp.float32)
    ahead = (lax.broadcasted_iota(jnp.int32, (8, 128), 0) + 1) % 4
    experts = (((x + ahead) % 4) * 2 + h).astype(jnp.float32)

    def route(meta):
        first, second = meta[0:1, :] == experts, meta[1:2, :] == experts
        named = jnp.where(first | second, 1.0, 0.0)
        weight = jnp.where(first, meta[2:3, :], 0.0) + jnp.where(second, meta[3:4, :], 0.0)
        rank = jnp.dot(named.astype(jnp.bfloat16), later, preferred_element_type=jnp.float32)
        picks = [jnp.where(place == rank[b:b + 1, :], named[b:b + 1, :], 0.0) for b in range(4)]
        return picks, [picks[b] * weight[b:b + 1, :] for b in range(4)]

    def dispatch(part, picks, source):
        chosen = jnp.concatenate(picks, axis=0).astype(jnp.bfloat16)

        def block(j, carry):
            cols = pl.ds(pl.multiple_of(j * 512, 512), 512)
            got = jnp.dot(chosen, source[pl.ds(0, 128), cols], preferred_element_type=jnp.float32).astype(jnp.bfloat16)
            for b in range(3):
                lanes[j, pl.ds(b * 160 + part * CAP, CAP), :] = got[b * CAP:(b + 1) * CAP]
            rows[j, pl.ds(480 + part * CAP, CAP), :] = got[3 * CAP:]
            return carry

        lax.fori_loop(0, 8, block, 0)
        ids = []
        for b in (0, 2, 1):
            at = pl.ds(b * 160 + part * CAP, CAP)
            ids.append((send(lanes.at[:, at, :], rows.at[:, at, :], x_by[b + 1]), at))
        return ids

    def block_of(r):
        return ((z + r // 2) % 4) * 2 + (y + r % 2) % 2

    def project(r, first, last):
        whole_slot(0, r)
        whole_slot(1, r)
        chip = block_of(r)

        def tile(n, carry):
            cols = pl.ds(pl.multiple_of(n * 256, 256), 256)
            seen = rows[chip]
            g = jnp.dot(seen, gate_buf[r, :, :, cols].reshape(512, 256), preferred_element_type=jnp.float32)
            u = jnp.dot(seen, up_buf[r, :, :, cols].reshape(512, 256), preferred_element_type=jnp.float32)
            if not first:
                g = gate_acc[:, cols] + g
                u = up_acc[:, cols] + u
            if last:
                hidden[:, cols] = (g / (1.0 + jnp.exp(-g)) * u).astype(jnp.bfloat16)
            else:
                gate_acc[:, cols] = g
                up_acc[:, cols] = u
            return carry

        lax.fori_loop(0, 6, tile, 0)

    homes = (own_tok, peer_tok, back)
    returns = {}

    def expand(g):
        whole_slot(2, g)

        def half(n, carry):
            cols = pl.ds(pl.multiple_of(n * 256, 256), 256)
            rows[g, :, cols] = jnp.dot(
                hidden[...], down_buf[g, n], preferred_element_type=jnp.float32).astype(jnp.bfloat16)
            return carry

        lax.fori_loop(0, 2, half, 0)
        returns[g] = []
        for b in (0, 2, 1):
            dst = homes[b].at[:, pl.ds(g * 512, 512)]
            returns[g].append((send(rows.at[g, pl.ds(b * 160, 160), :], dst, x_by[3 - b]), dst))

    parts = {}

    def combine(g):
        for i, dst in returns[g]:
            arrive(i, dst)
        total = 0.0
        for b in range(4):
            block = homes[b][:, pl.ds(g * 512, 512)] if b < 3 else rows[g, pl.ds(480, 160), :]
            for half in range(2):
                total = total + jnp.dot(mix[b, half], block, preferred_element_type=jnp.float32)
        gate_acc[pl.ds((g // 2) * 128, 128), pl.ds((g % 2) * 512, 512)] = total[:128]
        part_send[g] = total[128:].astype(jnp.bfloat16)
        parts[g] = send(part_send.at[g], part_recv.at[g ^ 1], y_out)

    def finish(g):
        arrive(parts[g ^ 1], part_recv.at[g])
        cols = pl.ds(pl.multiple_of(block_of(g) * 512, 512), 512)
        kept = gate_acc[pl.ds((g // 2) * 128, 128), pl.ds((g % 2) * 512, 512)]
        out_ref[:, cols] = (kept + part_recv[g].astype(jnp.float32)).astype(jnp.bfloat16)

    meta_id = send(meta_ref, peer_meta, y_out)
    tok_id = send(tok_hbm, peer_tok.at[pl.ds(0, 128), :], y_out)
    start_own(0)
    start_own(1)
    load_own.wait()
    picks, weighed = route(meta_ref[...])
    dispatched = dispatch(0, picks, own_tok)
    hop_two(0)
    arrive(meta_id, peer_meta)
    arrive(tok_id, peer_tok.at[pl.ds(0, 128), :])
    peer_picks, peer_weighed = route(peer_meta[...])
    dispatched += dispatch(1, peer_picks, peer_tok)
    hop_two(1)
    nothing = jnp.zeros((CAP, 128), jnp.float32)

    for b in range(4):
        whole = jnp.concatenate(
            [jnp.concatenate([weighed[b], nothing], axis=1),
             jnp.concatenate([nothing, peer_weighed[b]], axis=1)], axis=0).T
        high = whole.astype(jnp.bfloat16)
        mix[b, 0] = high
        mix[b, 1] = (whole - high.astype(jnp.float32)).astype(jnp.bfloat16)
    hop_three(0)
    start_own(2)
    hop_three(1)
    hop_four(0)
    for i, at in dispatched:
        arrive(i, rows.at[:, at, :])
    project(slot(0, 0), True, False)
    project(slot(0, 1), False, False)
    hop_two(2)
    hop_four(1)
    for r in (slot(3, 0), slot(1, 0), slot(2, 0), slot(3, 1), slot(1, 1)):
        project(r, False, False)
    project(slot(2, 1), False, True)
    expand(slot(0, 0))
    expand(slot(0, 1))
    hop_three(2)
    expand(slot(3, 0))
    expand(slot(1, 0))
    combine(slot(0, 0))
    expand(slot(2, 0))
    combine(slot(0, 1))
    expand(slot(3, 1))
    expand(slot(1, 1))
    combine(slot(3, 0))
    hop_four(2)
    expand(slot(2, 1))
    for g in (slot(1, 0), slot(2, 0), slot(3, 1), slot(1, 1), slot(2, 1)):
        combine(g)
    for g in (slot(0, 0), slot(0, 1), slot(3, 0), slot(1, 0), slot(2, 0), slot(3, 1), slot(1, 1), slot(2, 1)):
        finish(g)
    for copy in sends:
        copy.wait_send()


def on_device(tokens, expert_ids, gate_probs, gate_weight, up_weight, down_weight):
    meta = jnp.concatenate(
        [expert_ids.T.astype(jnp.float32), gate_probs.T, jnp.zeros((4, 128), jnp.float32)], axis=0)
    hbm, vmem = pl.BlockSpec(memory_space=pltpu.HBM), pl.BlockSpec(memory_space=pltpu.VMEM)
    return pl.pallas_call(
        kernel,
        out_shape=jax.ShapeDtypeStruct((128, 4096), jnp.bfloat16),
        in_specs=[hbm, vmem, hbm, hbm, hbm],
        out_specs=vmem,
        scratch_shapes=[
            pltpu.VMEM((8, 2, 256, 1536), jnp.bfloat16),
            pltpu.VMEM((8, 2, 256, 1536), jnp.bfloat16),
            pltpu.VMEM((8, 2, 1536, 256), jnp.bfloat16),
            pltpu.VMEM((640, 1536), jnp.float32),
            pltpu.VMEM((640, 1536), jnp.float32),
            pltpu.VMEM((8, 640, 512), jnp.bfloat16),
            pltpu.VMEM((640, 1536), jnp.bfloat16),
            pltpu.VMEM((160, 4096), jnp.bfloat16),
            pltpu.VMEM((160, 4096), jnp.bfloat16),
            pltpu.VMEM((8, 128), jnp.float32),
            pltpu.VMEM((160, 4096), jnp.bfloat16),
            pltpu.VMEM((8, 480, 512), jnp.bfloat16),
            pltpu.VMEM((8, 128, 512), jnp.bfloat16),
            pltpu.VMEM((8, 128, 512), jnp.bfloat16),
            pltpu.VMEM((4, 2, 256, 160), jnp.bfloat16),
            pltpu.SemaphoreType.DMA((COPIES,)),
            pltpu.SemaphoreType.DMA((COPIES,)),
            pltpu.SemaphoreType.DMA((4,)),
        ],
        compiler_params=pltpu.CompilerParams(
            collective_id=0, has_side_effects=True, vmem_limit_bytes=63 * 2**20),
        name="experts",
    )(tokens, meta, gate_weight, up_weight, down_weight)


def solution(mesh):
    placed = (
        P(("dp", "expert"), None),
        P(("dp", "expert"), None),
        P(("dp", "expert"), None),
        P("expert", "dp", None),
        P("expert", "dp", None),
        P("expert", None, "dp"),
    )
    return jax.shard_map(
        on_device, mesh=mesh, in_specs=placed, out_specs=P(("dp", "expert"), None), check_vma=False
    )
```

time: 432 us -> 197 us (0.46)
  waiting for transfers between devices: 255 us -> 0 us
  Pallas kernels: 0 us -> 193 us
  blocking collectives: 82.1 us -> 0 us
  matrix products: 41.9 us -> 0 us
  local copies, waits for them, and re-layouts: 20.8 us -> 3.64 us
  between operations: 13.2 us -> 0.01 us
  other arithmetic: 11.1 us -> 0.66 us
  starting transfers between devices: 6.92 us -> 0 us
    pallas_call x0 -> x1, Pallas kernels: none -> 193 us  [on_device(): pl.pallas_call(kernel, out_shape=jax.ShapeDtypeStruct((128, 4096), jnp.bf...]
    all_gather x3 -> x0, waiting for transfers between devices: 179 us -> none  [the longest x1 73.6 us: on_device(): lax.all_gather(up_local, 'dp', axis=0, tiled=True)]
    all_to_all x1 -> x0, blocking collectives: 82.1 us -> none  [on_device(): lax.all_to_all(send_rows, 'expert', split_axis=0, concat_axis=0, tiled=True)]
    all_to_all x1 -> x0, waiting for transfers between devices: 73.9 us -> none  [on_device(): lax.all_to_all(outputs, 'expert', split_axis=0, concat_axis=0, tiled=True)]
    dot_general x2 -> x0, matrix products: 41.9 us -> none  [the longest x1 27.9 us: on_device(): jnp.dot(hidden, lax.all_gather(down_local, 'dp', axis=1, tiled=True), pre...]
    gather x2 -> x0, local copies, waits for them, and re-layouts: 12.4 us -> none  [the longest x1 7.04 us: on_device(): picked = returned[slot_index].astype(jnp.float32)]
    reduce_sum x2 -> x0, other arithmetic: 9.72 us -> none  [the longest x1 9.64 us: on_device(): mixed = jnp.sum(weighted.reshape(tok_count, top_count, model_width), axis=1)]
    all_to_all x1 -> x0, starting transfers between devices: 6.84 us -> none  [on_device(): lax.all_to_all(outputs, 'expert', split_axis=0, concat_axis=0, tiled=True)]
  transfers between devices with their start and end apart: 4 -> 0, of which waited for: 4 -> 0; matrix products, arithmetic and copies ran while one was open for 6% -> 0% of each run, Pallas kernels for 0% -> 0%
where the time goes in v1:
time: 197 us
  Pallas kernels  193 us (98%)
  local copies, waits for them, and re-layouts  3.64 us (2%)
    pallas_call x1, Pallas kernels, on_device(): pl.pallas_call(kernel, out_shape=jax.ShapeDtypeStruct((128, 4096), jnp.bf...  193 us

profile of v1, /device:TPU:0, one launch (start us, length us, event | category | flops | bytes accessed | tf_op | source)
XLA Modules:
  0.0 196.8 jit_solution(15196471232663406708)
XLA Ops:
  0.0 0.0 copy-start
  0.0 0.1 pad.2.clone
  0.1 0.6 copy-done
  0.7 0.0 copy-start.1
  0.7 0.7 copy-done.1
  1.4 0.7 maximum_maximum_fusion.meta_ref
  2.0 192.5 %experts.1 = bf16[128,4096]{1,0:T(8,128)(2,1)} custom-call(bf16[128,4096]{1,0:T(8,128)(2,1)} %tok_hbm.1, f32[8,128]{1,0:T(8,128)} %maximum_maximum_fusion.meta_ref, bf16[1,256,1536]{2,1,0:T(8,128)(2,1)} %gate_hbm.1, bf16[1,256,1536]{2,1,0:T(8,128)(2,1)} %up_hbm.1, bf16[1,1536,256]{2,1,0:T(8,128)(2,1)} %down_hbm.1), custom_call_target="tpu_custom_call" | custom-call | tf_op jit(solution)/shard_map/experts/pallas_call | solution.py:284
  194.6 2.3 %copy.8 = bf16[128,4096]{1,0:T(8,128)(2,1)} copy(bf16[128,4096]{1,0:T(8,128)(2,1)} %experts.1) | data formatting | bytes 2097152
  (2 shorter events, 0.0 us)
Async XLA Ops:
  0.0 0.7 copy-start
  0.7 0.7 copy-start.1

commit v2 on v1

--- a/solution.py
+++ b/solution.py
@@ -15,7 +15,7 @@
 
 def kernel(tok_hbm, meta_ref, gate_hbm, up_hbm, down_hbm, out_ref,
            gate_buf, up_buf, down_buf, gate_acc, up_acc, rows, hidden, own_tok, peer_tok, peer_meta,
-           back, lanes, part_send, part_recv, mix, ssem, rsem, lsem):
+           back, lanes, part_recv, mix, ssem, rsem, lsem):
     dp = lax.axis_index("dp")
     ex = lax.axis_index("expert")
     core, y, z = dp % 2, (dp // 2) % 2, dp // 4
@@ -39,6 +39,7 @@
     pl.semaphore_wait(barrier, len(partners))
 
     sends = []
+    left = set()
 
     def send(src, dst, dev):
         i = len(sends)
@@ -77,43 +78,40 @@
         take(m, key, core)
         push(m, "s" + key, bufs[m].at[r, core], r, lo, hi, sibling)
 
-    def start_own(m):
-        n = sizes[m]
-        push(m, "y", args[m], slot(0, 1), 0, n, y_in)
-        push(m, "zu", args[m], slot(3, 0), 0, n, z_up)
-        push(m, "zd", args[m], slot(1, 0), 0, n, z_down)
-        push(m, "sown", args[m], slot(0, 0), 0, n, sibling)
+    def send_own(m, key):
+        r, dev = {"y": (slot(0, 1), y_in), "zu": (slot(3, 0), z_up), "zd": (slot(1, 0), z_down)}[key]
+        push(m, key, args[m], r, 0, sizes[m], dev)
+
+    def keep_own(m):
+        push(m, "sown", args[m], slot(0, 0), 0, sizes[m], sibling)
+
+    for m in range(3):
         copy = pltpu.make_async_copy(args[m], bufs[m].at[slot(0, 0), core], lsem.at[m])
         copy.start()
         local.append(copy)
 
-    def hop_two(m):
+    def relay_half(m, key):
         n = sizes[m]
-        cut = n - extra[m]
-        for key, dz, lo, hi, dev in (("zu", 3, 0, n // 2, z_up), ("zd", 1, n // 2, n, z_down)):
-            take(m, key, core)
-            src = bufs[m].at[slot(dz, 0), core]
-            push(m, "2" + key, src, slot(2, 0), lo, hi, dev)
-            push(m, "q" + key, src, slot(dz, 1), cut, n, y_in)
-            push(m, "s" + key, src, slot(dz, 0), 0, n, sibling)
+        dz, lo, hi, dev = {"zu": (3, 0, n // 2, z_up), "zd": (1, n // 2, n, z_down)}[key]
+        take(m, key, core)
+        src = bufs[m].at[slot(dz, 0), core]
+        push(m, "2" + key, src, slot(2, 0), lo, hi, dev)
+        push(m, "q" + key, src, slot(dz, 1), n - extra[m], n, y_in)
+        push(m, "s" + key, src, slot(dz, 0), 0, n, sibling)
+
+    def relay_peer(m):
+        n = sizes[m]
         take(m, "y", core)
         src = bufs[m].at[slot(0, 1), core]
-        push(m, "yzu", src, slot(3, 1), 0, cut, z_up)
-        push(m, "yzd", src, slot(1, 1), 0, cut, z_down)
+        push(m, "yzu", src, slot(3, 1), 0, n - extra[m], z_up)
+        push(m, "yzd", src, slot(1, 1), 0, n - extra[m], z_down)
         push(m, "sy", src, slot(0, 1), 0, n, sibling)
 
-    def hop_three(m):
-        for key in ("2zu", "2zd"):
-            i, r, lo, hi = events[m, key]
-            take(m, key, core)
-            push(m, "y" + key, bufs[m].at[r, core], slot(2, 1), lo, hi, y_in)
-            push(m, "s" + key, bufs[m].at[r, core], r, lo, hi, sibling)
-        for key in ("qzu", "qzd", "yzu", "yzd"):
-            pass_on(m, key)
-
-    def hop_four(m):
-        pass_on(m, "y2zu")
-        pass_on(m, "y2zd")
+    def relay_far(m, key):
+        i, r, lo, hi = events[m, key]
+        take(m, key, core)
+        push(m, "y" + key, bufs[m].at[r, core], slot(2, 1), lo, hi, y_in)
+        push(m, "s" + key, bufs[m].at[r, core], r, lo, hi, sibling)
 
     from_sibling = {
         slot(0, 0): ("sown",), slot(0, 1): ("sy",), slot(3, 0): ("szu",), slot(1, 0): ("szd",),
@@ -161,27 +159,40 @@
     def block_of(r):
         return ((z + r // 2) % 4) * 2 + (y + r % 2) % 2
 
-    def project(r, first, last):
-        whole_slot(0, r)
+    accs = (gate_acc, up_acc)
+
+    def clear():
+        gate_acc[...] = jnp.zeros_like(gate_acc)
+        up_acc[...] = jnp.zeros_like(up_acc)
+
+    def project(m, r):
+        whole_slot(m, r)
+        chip = block_of(r)
+        for n in range(2):
+            at = pl.ds(n * 320, 320)
+            accs[m][at, :] += jnp.dot(
+                rows[chip, at, :], bufs[m][r].reshape(512, 1536), preferred_element_type=jnp.float32)
+
+    def project_last(r):
         whole_slot(1, r)
-        chip = block_of(r)
 
         def tile(n, carry):
-            cols = pl.ds(pl.multiple_of(n * 256, 256), 256)
-            seen = rows[chip]
-            g = jnp.dot(seen, gate_buf[r, :, :, cols].reshape(512, 256), preferred_element_type=jnp.float32)
-            u = jnp.dot(seen, up_buf[r, :, :, cols].reshape(512, 256), preferred_element_type=jnp.float32)
-            if not first:
-                g = gate_acc[:, cols] + g
-                u = up_acc[:, cols] + u
-            if last:
-                hidden[:, cols] = (g / (1.0 + jnp.exp(-g)) * u).astype(jnp.bfloat16)
-            else:
-                gate_acc[:, cols] = g
-                up_acc[:, cols] = u
+            cols = pl.ds(pl.multiple_of(n * 512, 512), 512)
+            got = jnp.dot(
+                rows[block_of(r)], up_buf[r, :, :, cols].reshape(512, 512), preferred_element_type=jnp.float32)
+            hidden[:, cols] = (gate_acc[:, cols] * (up_acc[:, cols] + got)).astype(jnp.bfloat16)
             return carry
 
-        lax.fori_loop(0, 6, tile, 0)
+        lax.fori_loop(0, 3, tile, 0)
+
+    def activate():
+        def tile(n, carry):
+            at = pl.ds(pl.multiple_of(n * 32, 32), 32)
+            g = gate_acc[at, :]
+            gate_acc[at, :] = g / (1.0 + jnp.exp(-g))
+            return carry
+
+        lax.fori_loop(0, 20, tile, 0)
 
     homes = (own_tok, peer_tok, back)
     returns = {}
@@ -189,19 +200,16 @@
     def expand(g):
         whole_slot(2, g)
 
-        def half(n, carry):
-            cols = pl.ds(pl.multiple_of(n * 256, 256), 256)
-            rows[g, :, cols] = jnp.dot(
+        for n in range(2):
+            rows[g, :, pl.ds(n * 256, 256)] = jnp.dot(
                 hidden[...], down_buf[g, n], preferred_element_type=jnp.float32).astype(jnp.bfloat16)
-            return carry
-
-        lax.fori_loop(0, 2, half, 0)
         returns[g] = []
         for b in (0, 2, 1):
             dst = homes[b].at[:, pl.ds(g * 512, 512)]
             returns[g].append((send(rows.at[g, pl.ds(b * 160, 160), :], dst, x_by[3 - b]), dst))
 
     parts = {}
+    dispatched = []
 
     def combine(g):
         for i, dst in returns[g]:
@@ -212,8 +220,12 @@
             for half in range(2):
                 total = total + jnp.dot(mix[b, half], block, preferred_element_type=jnp.float32)
         gate_acc[pl.ds((g // 2) * 128, 128), pl.ds((g % 2) * 512, 512)] = total[:128]
-        part_send[g] = total[128:].astype(jnp.bfloat16)
-        parts[g] = send(part_send.at[g], part_recv.at[g ^ 1], y_out)
+        if not parts:
+            for i, at in dispatched:
+                sends[i].wait_send()
+                left.add(i)
+        lanes[g, pl.ds(0, 128), :] = total[128:].astype(jnp.bfloat16)
+        parts[g] = send(lanes.at[g, pl.ds(0, 128), :], part_recv.at[g ^ 1], y_out)
 
     def finish(g):
         arrive(parts[g ^ 1], part_recv.at[g])
@@ -221,60 +233,121 @@
         kept = gate_acc[pl.ds((g // 2) * 128, 128), pl.ds((g % 2) * 512, 512)]
         out_ref[:, cols] = (kept + part_recv[g].astype(jnp.float32)).astype(jnp.bfloat16)
 
+    def set_mix(weighed, peer_weighed):
+        nothing = jnp.zeros((CAP, 128), jnp.float32)
+        for b in range(4):
+            whole = jnp.concatenate(
+                [jnp.concatenate([weighed[b], nothing], axis=1),
+                 jnp.concatenate([nothing, peer_weighed[b]], axis=1)], axis=0).T
+            high = whole.astype(jnp.bfloat16)
+            mix[b, 0] = high
+            mix[b, 1] = (whole - high.astype(jnp.float32)).astype(jnp.bfloat16)
+
+    here, across, up1, down1 = slot(0, 0), slot(0, 1), slot(3, 0), slot(1, 0)
+    far, up2, down2, far2 = slot(2, 0), slot(3, 1), slot(1, 1), slot(2, 1)
+
     meta_id = send(meta_ref, peer_meta, y_out)
     tok_id = send(tok_hbm, peer_tok.at[pl.ds(0, 128), :], y_out)
-    start_own(0)
-    start_own(1)
+    send_own(0, "zd")
+    send_own(0, "zu")
+    send_own(1, "y")
     load_own.wait()
     picks, weighed = route(meta_ref[...])
-    dispatched = dispatch(0, picks, own_tok)
-    hop_two(0)
+    dispatched += dispatch(0, picks, own_tok)
+    clear()
+    send_own(1, "zd")
+    send_own(0, "y")
+    keep_own(1)
+    send_own(1, "zu")
+    relay_half(0, "zd")
+    relay_half(0, "zu")
+    relay_half(1, "zu")
     arrive(meta_id, peer_meta)
     arrive(tok_id, peer_tok.at[pl.ds(0, 128), :])
     peer_picks, peer_weighed = route(peer_meta[...])
     dispatched += dispatch(1, peer_picks, peer_tok)
-    hop_two(1)
-    nothing = jnp.zeros((CAP, 128), jnp.float32)
-
-    for b in range(4):
-        whole = jnp.concatenate(
-            [jnp.concatenate([weighed[b], nothing], axis=1),
-             jnp.concatenate([nothing, peer_weighed[b]], axis=1)], axis=0).T
-        high = whole.astype(jnp.bfloat16)
-        mix[b, 0] = high
-        mix[b, 1] = (whole - high.astype(jnp.float32)).astype(jnp.bfloat16)
-    hop_three(0)
-    start_own(2)
-    hop_three(1)
-    hop_four(0)
+    set_mix(weighed, peer_weighed)
+    relay_half(1, "zd")
+    relay_far(0, "2zd")
+    relay_peer(0)
+    pass_on(0, "qzu")
+    relay_far(0, "2zu")
+    relay_far(1, "2zd")
+    relay_peer(1)
+    keep_own(2)
+    keep_own(0)
     for i, at in dispatched:
         arrive(i, rows.at[:, at, :])
-    project(slot(0, 0), True, False)
-    project(slot(0, 1), False, False)
-    hop_two(2)
-    hop_four(1)
-    for r in (slot(3, 0), slot(1, 0), slot(2, 0), slot(3, 1), slot(1, 1)):
-        project(r, False, False)
-    project(slot(2, 1), False, True)
-    expand(slot(0, 0))
-    expand(slot(0, 1))
-    hop_three(2)
-    expand(slot(3, 0))
-    expand(slot(1, 0))
-    combine(slot(0, 0))
-    expand(slot(2, 0))
-    combine(slot(0, 1))
-    expand(slot(3, 1))
-    expand(slot(1, 1))
-    combine(slot(3, 0))
-    hop_four(2)
-    expand(slot(2, 1))
-    for g in (slot(1, 0), slot(2, 0), slot(3, 1), slot(1, 1), slot(2, 1)):
-        combine(g)
-    for g in (slot(0, 0), slot(0, 1), slot(3, 0), slot(1, 0), slot(2, 0), slot(3, 1), slot(1, 1), slot(2, 1)):
-        finish(g)
-    for copy in sends:
-        copy.wait_send()
+    relay_far(1, "2zu")
+    project(0, here)
+    project(1, far)
+    pass_on(0, "y2zu")
+    project(1, up1)
+    project(1, across)
+    pass_on(1, "qzd")
+    project(0, up1)
+    project(1, down1)
+    pass_on(0, "yzd")
+    pass_on(0, "yzu")
+    send_own(2, "zd")
+    project(1, here)
+    pass_on(1, "y2zd")
+    send_own(2, "y")
+    pass_on(0, "qzd")
+    pass_on(0, "y2zd")
+    pass_on(1, "qzu")
+    project(0, far)
+    project(0, up2)
+    send_own(2, "zu")
+    project(0, across)
+    project(0, down2)
+    project(0, far2)
+    pass_on(1, "y2zu")
+    project(0, down1)
+    pass_on(1, "yzu")
+    pass_on(1, "yzd")
+    project(1, far2)
+    project(1, up2)
+    activate()
+    project_last(down2)
+    expand(here)
+    relay_half(2, "zd")
+    relay_half(2, "zu")
+    relay_peer(2)
+    expand(down1)
+    expand(up1)
+    relay_far(2, "2zd")
+    expand(across)
+    relay_far(2, "2zu")
+    pass_on(2, "yzd")
+    expand(far)
+    combine(across)
+    pass_on(2, "qzd")
+    pass_on(2, "qzu")
+    expand(down2)
+    pass_on(2, "y2zu")
+    combine(down1)
+    pass_on(2, "y2zd")
+    combine(far)
+    combine(here)
+    combine(up1)
+    expand(far2)
+    pass_on(2, "yzu")
+    combine(down2)
+    expand(up2)
+    finish(here)
+    finish(down1)
+    combine(far2)
+    finish(across)
+    combine(up2)
+    finish(down2)
+    finish(up2)
+    finish(far)
+    finish(far2)
+    finish(up1)
+    for i, copy in enumerate(sends):
+        if i not in left:
+            copy.wait_send()
 
 
 def on_device(tokens, expert_ids, gate_probs, gate_weight, up_weight, down_weight):
@@ -300,7 +373,6 @@
             pltpu.VMEM((160, 4096), jnp.bfloat16),
             pltpu.VMEM((8, 480, 512), jnp.bfloat16),
             pltpu.VMEM((8, 128, 512), jnp.bfloat16),
-            pltpu.VMEM((8, 128, 512), jnp.bfloat16),
             pltpu.VMEM((4, 2, 256, 160), jnp.bfloat16),
             pltpu.SemaphoreType.DMA((COPIES,)),
             pltpu.SemaphoreType.DMA((COPIES,)),

time: 197 us -> 172 us (0.87)
  Pallas kernels: 193 us -> 167 us
    pallas_call x1, Pallas kernels: 193 us -> 167 us  [on_device(): pl.pallas_call(kernel, out_shape=jax.ShapeDtypeStruct((128, 4096), jnp.bf...]
where the time goes in v2:
time: 172 us; the launch traced here: 171 us
  Pallas kernels  167 us (97%)
  local copies, waits for them, and re-layouts  3.64 us (2%)
    pallas_call x1, Pallas kernels, on_device(): pl.pallas_call(kernel, out_shape=jax.ShapeDtypeStruct((128, 4096), jnp.bf...  167 us
    unnamed x5, local copies, waits for them, and re-layouts  3.57 us

profile of v2, /device:TPU:0, one launch (start us, length us, event | category | flops | bytes accessed | tf_op | source)
XLA Modules:
  0.0 171.3 jit_solution(11736784673140022890)
XLA Ops:
  0.0 0.0 copy-start
  0.0 0.1 pad.2.clone
  0.1 0.6 copy-done
  0.7 0.0 copy-start.1
  0.7 0.7 copy-done.1
  1.4 0.7 maximum_maximum_fusion.meta_ref
  2.0 167.0 %experts.1 = bf16[128,4096]{1,0:T(8,128)(2,1)} custom-call(bf16[128,4096]{1,0:T(8,128)(2,1)} %tok_hbm.1, f32[8,128]{1,0:T(8,128)} %maximum_maximum_fusion.meta_ref, bf16[1,256,1536]{2,1,0:T(8,128)(2,1)} %gate_hbm.1, bf16[1,256,1536]{2,1,0:T(8,128)(2,1)} %up_hbm.1, bf16[1,1536,256]{2,1,0:T(8,128)(2,1)} %down_hbm.1), custom_call_target="tpu_custom_call" | custom-call | tf_op jit(solution)/shard_map/experts/pallas_call | solution.py:357
  169.0 2.3 %copy.8 = bf16[128,4096]{1,0:T(8,128)(2,1)} copy(bf16[128,4096]{1,0:T(8,128)(2,1)} %experts.1) | data formatting | bytes 2097152
  (2 shorter events, 0.0 us)
Async XLA Ops:
  0.0 0.7 copy-start
  0.7 0.7 copy-start.1

commit v3 on v2

--- a/solution.py
+++ b/solution.py
@@ -13,9 +13,9 @@
     return (dz % 4) * 2 + dy
 
 
-def kernel(tok_hbm, meta_ref, gate_hbm, up_hbm, down_hbm, out_ref,
-           gate_buf, up_buf, down_buf, gate_acc, up_acc, rows, hidden, own_tok, peer_tok, peer_meta,
-           back, lanes, part_recv, mix, ssem, rsem, lsem):
+def kernel(tok_hbm, ids_ref, probs_ref, gate_hbm, up_hbm, down_hbm, kept_hbm, peer_hbm,
+           gate_buf, up_buf, down_buf, gate_acc, up_acc, rows, hidden, own_tok, peer_tok, meta_ref, peer_meta,
+           back, lanes, mix, ssem, rsem, lsem):
     dp = lax.axis_index("dp")
     ex = lax.axis_index("expert")
     core, y, z = dp % 2, (dp // 2) % 2, dp // 4
@@ -34,6 +34,8 @@
     barrier = pltpu.get_barrier_semaphore()
     load_own = pltpu.make_async_copy(tok_hbm, own_tok.at[pl.ds(0, 128), :], lsem.at[3])
     load_own.start()
+    meta_ref[pl.ds(0, 2), :] = ids_ref[...].astype(jnp.float32)
+    meta_ref[pl.ds(2, 2), :] = probs_ref[...]
     for partner in partners:
         pl.semaphore_signal(barrier, inc=1, device_id=partner, device_id_type=MESH)
     pl.semaphore_wait(barrier, len(partners))
@@ -209,7 +211,11 @@
             returns[g].append((send(rows.at[g, pl.ds(b * 160, 160), :], dst, x_by[3 - b]), dst))
 
     parts = {}
-    dispatched = []
+    dispatched, keeps = [], []
+
+    def columns(g):
+        return pl.ds(pl.multiple_of(block_of(g) * 512, 512), 512)
+
 
     def combine(g):
         for i, dst in returns[g]:
@@ -219,19 +225,23 @@
             block = homes[b][:, pl.ds(g * 512, 512)] if b < 3 else rows[g, pl.ds(480, 160), :]
             for half in range(2):
                 total = total + jnp.dot(mix[b, half], block, preferred_element_type=jnp.float32)
-        gate_acc[pl.ds((g // 2) * 128, 128), pl.ds((g % 2) * 512, 512)] = total[:128]
+        kept = (pl.ds((g // 2) * 128, 128), pl.ds((g % 2) * 512, 512))
+        gate_acc[kept] = total[:128]
+        copy = pltpu.make_async_copy(gate_acc.at[kept], kept_hbm.at[:, columns(g)], lsem.at[4 + g])
+        copy.start()
+        keeps.append(copy)
         if not parts:
             for i, at in dispatched:
                 sends[i].wait_send()
                 left.add(i)
         lanes[g, pl.ds(0, 128), :] = total[128:].astype(jnp.bfloat16)
-        parts[g] = send(lanes.at[g, pl.ds(0, 128), :], part_recv.at[g ^ 1], y_out)
-
-    def finish(g):
-        arrive(parts[g ^ 1], part_recv.at[g])
-        cols = pl.ds(pl.multiple_of(block_of(g) * 512, 512), 512)
-        kept = gate_acc[pl.ds((g // 2) * 128, 128), pl.ds((g % 2) * 512, 512)]
-        out_ref[:, cols] = (kept + part_recv[g].astype(jnp.float32)).astype(jnp.bfloat16)
+        parts[g] = send(lanes.at[g, pl.ds(0, 128), :], peer_hbm.at[:, columns(g)], y_out)
+
+    def finish():
+        for g in range(8):
+            arrive(parts[g], peer_hbm.at[:, columns(g ^ 1)])
+        for copy in keeps:
+            copy.wait()
 
     def set_mix(weighed, peer_weighed):
         nothing = jnp.zeros((CAP, 128), jnp.float32)
@@ -335,30 +345,21 @@
     pass_on(2, "yzu")
     combine(down2)
     expand(up2)
-    finish(here)
-    finish(down1)
     combine(far2)
-    finish(across)
     combine(up2)
-    finish(down2)
-    finish(up2)
-    finish(far)
-    finish(far2)
-    finish(up1)
+    finish()
     for i, copy in enumerate(sends):
         if i not in left:
             copy.wait_send()
 
 
 def on_device(tokens, expert_ids, gate_probs, gate_weight, up_weight, down_weight):
-    meta = jnp.concatenate(
-        [expert_ids.T.astype(jnp.float32), gate_probs.T, jnp.zeros((4, 128), jnp.float32)], axis=0)
     hbm, vmem = pl.BlockSpec(memory_space=pltpu.HBM), pl.BlockSpec(memory_space=pltpu.VMEM)
-    return pl.pallas_call(
+    kept, peer = pl.pallas_call(
         kernel,
-        out_shape=jax.ShapeDtypeStruct((128, 4096), jnp.bfloat16),
-        in_specs=[hbm, vmem, hbm, hbm, hbm],
-        out_specs=vmem,
+        out_shape=(jax.ShapeDtypeStruct((128, 4096), jnp.float32), jax.ShapeDtypeStruct((128, 4096), jnp.bfloat16)),
+        in_specs=[hbm, vmem, vmem, hbm, hbm, hbm],
+        out_specs=(hbm, hbm),
         scratch_shapes=[
             pltpu.VMEM((8, 2, 256, 1536), jnp.bfloat16),
             pltpu.VMEM((8, 2, 256, 1536), jnp.bfloat16),
@@ -370,18 +371,19 @@
             pltpu.VMEM((160, 4096), jnp.bfloat16),
             pltpu.VMEM((160, 4096), jnp.bfloat16),
             pltpu.VMEM((8, 128), jnp.float32),
+            pltpu.VMEM((8, 128), jnp.float32),
             pltpu.VMEM((160, 4096), jnp.bfloat16),
             pltpu.VMEM((8, 480, 512), jnp.bfloat16),
-            pltpu.VMEM((8, 128, 512), jnp.bfloat16),
             pltpu.VMEM((4, 2, 256, 160), jnp.bfloat16),
             pltpu.SemaphoreType.DMA((COPIES,)),
             pltpu.SemaphoreType.DMA((COPIES,)),
-            pltpu.SemaphoreType.DMA((4,)),
+            pltpu.SemaphoreType.DMA((12,)),
         ],
         compiler_params=pltpu.CompilerParams(
             collective_id=0, has_side_effects=True, vmem_limit_bytes=63 * 2**20),
         name="experts",
-    )(tokens, meta, gate_weight, up_weight, down_weight)
+    )(tokens, expert_ids.T, gate_probs.T, gate_weight, up_weight, down_weight)
+    return (kept + peer.astype(jnp.float32)).astype(jnp.bfloat16)
 
 
 def solution(mesh):

time: 172 us -> 169 us (0.983)
  local copies, waits for them, and re-layouts: 3.64 us -> 0 us
  other arithmetic: 0.66 us -> 3.04 us
    unnamed x5 -> x0, local copies, waits for them, and re-layouts: 3.57 us -> none
    convert_element_type x1, other arithmetic: 0.01 us -> 3.04 us  [on_device(): return (kept + peer.astype(jnp.float32)).astype(jnp.bfloat16)]
where the time goes in v3:
time: 169 us
  Pallas kernels  166 us (98%)
  other arithmetic  3.04 us (2%)
    pallas_call x1, Pallas kernels, on_device(): pl.pallas_call(kernel, out_shape=(jax.ShapeDtypeStruct((128, 4096), jnp.f...  166 us

profile of v3, /device:TPU:0, one launch (start us, length us, event | category | flops | bytes accessed | tf_op | source)
XLA Modules:
  0.0 169.2 jit_solution(12310995323681833909)
XLA Ops:
  0.0 166.2 %experts.1 = (f32[128,4096]{1,0:T(8,128)}, bf16[128,4096]{1,0:T(8,128)(2,1)}) custom-call(bf16[128,4096]{1,0:T(8,128)(2,1)} %tok_hbm.1, s32[2,128]{1,0:T(2,128)} %bitcast.2, f32[2,128]{1,0:T(2,128)} %bitcast.3, bf16[1,256,1536]{2,1,0:T(8,128)(2,1)} %gate_hbm.1, bf16[1,256,1536]{2,1,0:T(8,128)(2,1)} %up_hbm.1, bf16[1,1536,256]{2,1,0:T(8,128)(2,1)} %down_hbm.1), custom_call_target="tpu_custom_call" | custom-call | tf_op jit(solution)/shard_map/experts/pallas_call | solution.py:358
  166.2 3.0 %add_convert_fusion = bf16[128,4096]{1,0:T(8,128)(2,1)} fusion(f32[128,4096]{1,0:T(8,128)} %get-tuple-element.7, bf16[128,4096]{1,0:T(8,128)(2,1)} %get-tuple-element.8), kind=kLoop, calls=%fused_computation | loop fusion | flops 1572864 | bytes 4194304 | tf_op jit(solution)/shard_map/convert_element_type | solution.py:386

commit v4 on v3

--- a/solution.py
+++ b/solution.py
@@ -13,7 +13,7 @@
     return (dz % 4) * 2 + dy
 
 
-def kernel(tok_hbm, ids_ref, probs_ref, gate_hbm, up_hbm, down_hbm, kept_hbm, peer_hbm,
+def kernel(tok_hbm, ids_ref, probs_ref, gate_hbm, up_hbm, down_hbm, kept_ref, peer_ref,
            gate_buf, up_buf, down_buf, gate_acc, up_acc, rows, hidden, own_tok, peer_tok, meta_ref, peer_meta,
            back, lanes, mix, ssem, rsem, lsem):
     dp = lax.axis_index("dp")
@@ -211,7 +211,7 @@
             returns[g].append((send(rows.at[g, pl.ds(b * 160, 160), :], dst, x_by[3 - b]), dst))
 
     parts = {}
-    dispatched, keeps = [], []
+    dispatched = []
 
     def columns(g):
         return pl.ds(pl.multiple_of(block_of(g) * 512, 512), 512)
@@ -225,23 +225,17 @@
             block = homes[b][:, pl.ds(g * 512, 512)] if b < 3 else rows[g, pl.ds(480, 160), :]
             for half in range(2):
                 total = total + jnp.dot(mix[b, half], block, preferred_element_type=jnp.float32)
-        kept = (pl.ds((g // 2) * 128, 128), pl.ds((g % 2) * 512, 512))
-        gate_acc[kept] = total[:128]
-        copy = pltpu.make_async_copy(gate_acc.at[kept], kept_hbm.at[:, columns(g)], lsem.at[4 + g])
-        copy.start()
-        keeps.append(copy)
+        kept_ref[:, columns(g)] = total[:128].astype(jnp.bfloat16)
         if not parts:
             for i, at in dispatched:
                 sends[i].wait_send()
                 left.add(i)
         lanes[g, pl.ds(0, 128), :] = total[128:].astype(jnp.bfloat16)
-        parts[g] = send(lanes.at[g, pl.ds(0, 128), :], peer_hbm.at[:, columns(g)], y_out)
+        parts[g] = send(lanes.at[g, pl.ds(0, 128), :], peer_ref.at[:, columns(g)], y_out)
 
     def finish():
         for g in range(8):
-            arrive(parts[g], peer_hbm.at[:, columns(g ^ 1)])
-        for copy in keeps:
-            copy.wait()
+            arrive(parts[g], peer_ref.at[:, columns(g ^ 1)])
 
     def set_mix(weighed, peer_weighed):
         nothing = jnp.zeros((CAP, 128), jnp.float32)
@@ -357,9 +351,9 @@
     hbm, vmem = pl.BlockSpec(memory_space=pltpu.HBM), pl.BlockSpec(memory_space=pltpu.VMEM)
     kept, peer = pl.pallas_call(
         kernel,
-        out_shape=(jax.ShapeDtypeStruct((128, 4096), jnp.float32), jax.ShapeDtypeStruct((128, 4096), jnp.bfloat16)),
+        out_shape=(jax.ShapeDtypeStruct((128, 4096), jnp.bfloat16), jax.ShapeDtypeStruct((128, 4096), jnp.bfloat16)),
         in_specs=[hbm, vmem, vmem, hbm, hbm, hbm],
-        out_specs=(hbm, hbm),
+        out_specs=(vmem, vmem),
         scratch_shapes=[
             pltpu.VMEM((8, 2, 256, 1536), jnp.bfloat16),
             pltpu.VMEM((8, 2, 256, 1536), jnp.bfloat16),
@@ -377,13 +371,13 @@
             pltpu.VMEM((4, 2, 256, 160), jnp.bfloat16),
             pltpu.SemaphoreType.DMA((COPIES,)),
             pltpu.SemaphoreType.DMA((COPIES,)),
-            pltpu.SemaphoreType.DMA((12,)),
+            pltpu.SemaphoreType.DMA((4,)),
         ],
         compiler_params=pltpu.CompilerParams(
             collective_id=0, has_side_effects=True, vmem_limit_bytes=63 * 2**20),
         name="experts",
     )(tokens, expert_ids.T, gate_probs.T, gate_weight, up_weight, down_weight)
-    return (kept + peer.astype(jnp.float32)).astype(jnp.bfloat16)
+    return (kept.astype(jnp.float32) + peer.astype(jnp.float32)).astype(jnp.bfloat16)
 
 
 def solution(mesh):

time: 169 us -> 170 us (level)
  no operation moved by 1% of the time
where the time goes in v4:
time: 170 us
  Pallas kernels  167 us (98%)
  other arithmetic  2.76 us (2%)
    pallas_call x1, Pallas kernels, on_device(): pl.pallas_call(kernel, out_shape=(jax.ShapeDtypeStruct((128, 4096), jnp.b...  167 us

profile of v4, /device:TPU:0, one launch (start us, length us, event | category | flops | bytes accessed | tf_op | source)
XLA Modules:
  0.0 170.1 jit_solution(1052101609186797270)
XLA Ops:
  0.0 167.4 %experts.1 = (bf16[128,4096]{1,0:T(8,128)(2,1)}, bf16[128,4096]{1,0:T(8,128)(2,1)}) custom-call(bf16[128,4096]{1,0:T(8,128)(2,1)} %tok_hbm.1, s32[2,128]{1,0:T(2,128)} %bitcast.2, f32[2,128]{1,0:T(2,128)} %bitcast.3, bf16[1,256,1536]{2,1,0:T(8,128)(2,1)} %gate_hbm.1, bf16[1,256,1536]{2,1,0:T(8,128)(2,1)} %up_hbm.1, bf16[1,1536,256]{2,1,0:T(8,128)(2,1)} %down_hbm.1), custom_call_target="tpu_custom_call" | custom-call | tf_op jit(solution)/shard_map/experts/pallas_call | solution.py:352
  167.4 2.8 %add_convert_fusion = bf16[128,4096]{1,0:T(8,128)(2,1)} fusion(bf16[128,4096]{1,0:T(8,128)(2,1)} %get-tuple-element.8, bf16[128,4096]{1,0:T(8,128)(2,1)} %get-tuple-element.7), kind=kLoop, calls=%fused_computation | loop fusion | flops 2097152 | bytes 3145728 | tf_op jit(solution)/shard_map/convert_element_type | solution.py:380
